TPU v7x, 128 devices: a whole 4x4x4 slice. The times are simulated.
128 devices in a mesh: rep: 4 (over z_lo, core), blk: 32 (over y, x, z_hi).
Axes of the slice: x: 4, y: 4, z: 4 (z_hi: 2, z_lo: 2; z = z_hi * 2 + z_lo), core: 2. Of those that a mesh axis runs over, the one named last changes fastest.
Arguments:
- features: bfloat16 [262144, 256], P(('blk', 'rep')), may hold values from -6 to 6
- restriction: float32 [64, 16, 16], replicated, may hold values from -1.5 to 1.5
- mixing: float32 [16, 16], replicated, may hold values from -1.5 to 1.5
- source_index: int32 [32, 4, 2, 2048], P('blk', 'rep'), may hold values from 0 to 8191
- target_index: int32 [32, 4, 2, 2048], P('blk', 'rep'), may hold values from 0 to 8191
- map_index: int32 [32, 4, 2, 2048], P('blk', 'rep'), may hold values from 0 to 63
- edge_counts: int32 [32, 4, 2], P('blk', 'rep'), may hold values from 32 to 2048, as said below
Outputs:
- updated: bfloat16 [262144, 256], P(('blk', 'rep'))
Inputs may be any that keep to these rules, and one draw needn't show every extreme that they name: `edge_counts`: each count is max(1, 2048 * l * l // 64) for a whole l from 1 to 8; some tile has exactly 2048 live slots in every draw.
All inputs are finite; a program needn't handle non-finite values.
Results may differ from a plain program's by a relative error of at most 0.0034.
Values may be sent and summed in bfloat16 or wider, within the bound.
A program may use at most 128 MiB of HBM per device.

v0:
```python
import jax
import jax.numpy as jnp
from jax import lax
from jax.sharding import PartitionSpec as P


def passed_along(block, axis, distance):
    devices = range(lax.axis_size(axis))
    route = [((i - distance) % len(devices), i) for i in devices]
    return lax.ppermute(block, axis, route)


def body(features, restriction, mixing, source_index, target_index, map_index, edge_counts):
    node_rows = features.shape[0]
    feature_width = features.shape[1]
    replicas = lax.axis_size("rep")
    block_rows = node_rows * replicas
    stalk = restriction.shape[1]
    channels = mixing.shape[0]
    capacity = source_index.shape[3]
    cycle_turns = source_index.shape[2]
    edge_block = min(capacity, 1024)
    partial_value = jnp.zeros((block_rows, feature_width), jnp.float32)
    all_sources = source_index[0]
    all_targets = target_index[0]
    all_maps = map_index[0]
    all_counts = edge_counts[0]
    source_block = lax.all_gather(features, "rep", axis=0, tiled=True)
    for cycle_turn in range(cycle_turns):
        if cycle_turn > 0:
            source_block = passed_along(source_block, "blk", 1)
        sources = all_sources[:, cycle_turn]
        targets = all_targets[:, cycle_turn]
        maps = all_maps[:, cycle_turn]
        counts = all_counts[:, cycle_turn]
        out_rows = partial_value.shape[0]
        node_ids = lax.broadcasted_iota(jnp.int32, (out_rows, edge_block), 0)
        groups = sources.shape[0]

        def over_group(group, totals):
            group_sources = lax.dynamic_index_in_dim(sources, group, 0, keepdims=False)
            group_targets = lax.dynamic_index_in_dim(targets, group, 0, keepdims=False)
            group_maps = lax.dynamic_index_in_dim(maps, group, 0, keepdims=False)
            live_count = lax.dynamic_index_in_dim(counts, group, 0, keepdims=False)

            def add_block(block_number, inner):
                first_edge = block_number * edge_block
                source_part = lax.dynamic_slice_in_dim(group_sources, first_edge, edge_block)
                target_part = lax.dynamic_slice_in_dim(group_targets, first_edge, edge_block)
                map_part = lax.dynamic_slice_in_dim(group_maps, first_edge, edge_block)
                gathered = (
                    jnp.take(source_block, source_part, axis=0)
                    .astype(jnp.float32)
                    .reshape(edge_block, stalk, channels)
                )
                chosen = jnp.take(restriction, map_part, axis=0)
                message = jnp.einsum(
                    "eij,ejc->eic", chosen, gathered, precision=lax.Precision.HIGHEST
                )
                message = message.reshape(edge_block, feature_width).astype(jnp.bfloat16)
                positions = first_edge + lax.broadcasted_iota(jnp.int32, (1, edge_block), 1)
                selector = ((target_part[None, :] == node_ids) & (positions < live_count)).astype(
                    jnp.bfloat16
                )
                return inner + jnp.dot(selector, message, preferred_element_type=jnp.float32)

            upper = capacity // edge_block
            return lax.fori_loop(0, upper, add_block, totals)

        partial_value = lax.fori_loop(0, groups, over_group, partial_value)
    summed = lax.psum_scatter(partial_value, "rep", scatter_dimension=0, tiled=True)
    spread = jnp.kron(jnp.eye(stalk, dtype=jnp.float32), mixing)
    mixed = jnp.dot(
        summed, spread, precision=lax.Precision.HIGHEST, preferred_element_type=jnp.float32
    )
    return (features.astype(jnp.float32) + mixed).astype(jnp.bfloat16)


def solution(mesh):
    in_specs = (
        P(("blk", "rep"), None),
        P(),
        P(),
        P("blk", "rep", None, None),
        P("blk", "rep", None, None),
        P("blk", "rep", None, None),
        P("blk", "rep", None),
    )
    out_specs = P(("blk", "rep"), None)
    return jax.shard_map(body, mesh=mesh, in_specs=in_specs, out_specs=out_specs, check_vma=False)
```

profile of v0, /device:TPU:1, one launch (start us, length us, event | category | flops | bytes accessed | tf_op | source)
XLA Modules:
  0.0 347.1 jit_solution(11246119724384150973)
XLA Ops:
  7.3 1.2 copy.16
  8.5 1.4 fusion.45
  12.3 46.9 %all-gather.2.cloned.1.call-done = bf16[8192,256]{1,0:T(8,128)(2,1)} async-done(((bf16[2048,256]{1,0:T(8,128)(2,1)}), bf16[8192,256]{1,0:T(8,128)(2,1)}) %all-gather.2.cloned.1.call-update) | async-done | bytes 4194320 | tf_op jit(solution)/shard_map/all_gather | solution.py:28
  59.2 2.6 collective-permute-start
  61.8 96.8 %while.45 = (s32[]{:T(128)}, f32[8192,256]{1,0:T(8,128)}, s32[2048]{0:T(1024)S(1)}, s32[]{:T(128)}, s32[2048]{0:T(1024)S(1)}, /*index=5*/f32[64,16,16]{2,1,0:T(8...) while((s32[]{:T(128)}, f32[8192,256]{1,0:T(8,128)}, ...), condition=%wide.region_1.4_spmd.clone, body=%wide.region_0.3_spmd.clone.sunk | while | flops 4367079424 | bytes 26790084 | solution.py:68
  62.5 6.2 %gather_fusion.2 = bf16[1024,256]{1,0:T(8,128)(2,1)S(1)} fusion(bf16[8192,256]{1,0:T(8,128)(2,1)} %get-tuple-element.655, s32[1024]{0:T(1024)S(1)} %get-tuple-element.620), kind=kCustom, calls=%fused_computation.1.clone.clone.1 | custom fusion | bytes 1052672 | tf_op jit(solution)/shard_map/while/body/eval_jaxpr/while/body/eval_jaxpr/jit(_take)/gather | solution.py:52
  69.1 4.8 %copy.28 = bf16[1024,16,16]{2,1,0:T(8,128)(2,1)} copy(bf16[1024,16,16]{0,2,1:T(8,128)(2,1)S(1)} %bitcast.40) | data formatting | bytes 1048576 | tf_op jit(solution)/shard_map/while/body/eval_jaxpr/while/body/eval_jaxpr/reshape | solution.py:54
  73.9 10.6 %gather_fusion.3 = f32[1024,16,16]{2,1,0:T(8,128)} fusion(f32[64,16,16]{2,1,0:T(8,128)S(1)} %get-tuple-element.653, s32[1024]{0:T(1024)S(1)} %get-tuple-element.622), kind=kCustom, calls=%fused_computation.clone.clone.1 | custom fusion | bytes 2101248 | tf_op jit(solution)/shard_map/while/body/eval_jaxpr/while/body/eval_jaxpr/jit(_take)/gather | solution.py:56
  84.6 10.4 %fusion.78 = bf16[1024,16,16]{2,1,0:T(8,128)(2,1)} fusion(bf16[1024,16,16]{2,1,0:T(8,128)(2,1)} %copy.28, f32[1024,16,16]{2,1,0:T(8,128)} %gather_fusion.3, pred[1024]{0:T(1024)(128)(4,1)S(1)} %compare_and_fusion.7), kind=kOutput, calls=%fused_computation.36.clone.1 | convolution fusion | flops 50855936 | bytes 2098176 | tf_op jit(solution)/shard_map/while/body/eval_jaxpr/while/body/eval_jaxpr/eij,ejc->eic/dot_general | solution.py:57
  94.9 4.4 %copy.29 = bf16[1024,16,16]{0,2,1:T(8,128)(2,1)S(1)} copy(bf16[1024,16,16]{2,1,0:T(8,128)(2,1)} %fusion.78) | data formatting | bytes 1048576 | tf_op jit(solution)/shard_map/while/body/eval_jaxpr/while/body/eval_jaxpr/convert_element_type | solution.py:60
  99.4 9.8 %fusion.79 = f32[8192,256]{1,0:T(8,128)} fusion(bf16[1024,256]{0,1:T(8,128)(2,1)S(1)} %bitcast.42, s32[1024]{0:T(1024)S(1)} %dynamic_slice.97, pred[1024]{0:T(1024)(128)(4,1)S(1)} %get-tuple-element.623, f32[8192,256]{1,0:T(8,128)} %get-tuple-element.637, pred[]{:T(512)S(6)} %compare.3), kind=kOutput, calls=%fused_computation.31.clone.1 | convolution fusion | flops 4315938816 | bytes 17306624 | tf_op jit(solution)/shard_map/while/body/eval_jaxpr/while/body/eval_jaxpr/dot_general | solution.py:65
  109.9 6.2 %gather_fusion.2 = bf16[1024,256]{1,0:T(8,128)(2,1)S(1)} fusion(bf16[8192,256]{1,0:T(8,128)(2,1)} %get-tuple-element.655, s32[1024]{0:T(1024)S(1)} %get-tuple-element.620), kind=kCustom, calls=%fused_computation.1.clone.clone.1 | custom fusion | bytes 1052672 | tf_op jit(solution)/shard_map/while/body/eval_jaxpr/while/body/eval_jaxpr/jit(_take)/gather | solution.py:52
  116.5 4.8 %copy.28 = bf16[1024,16,16]{2,1,0:T(8,128)(2,1)} copy(bf16[1024,16,16]{0,2,1:T(8,128)(2,1)S(1)} %bitcast.40) | data formatting | bytes 1048576 | tf_op jit(solution)/shard_map/while/body/eval_jaxpr/while/body/eval_jaxpr/reshape | solution.py:54
  121.3 10.6 %gather_fusion.3 = f32[1024,16,16]{2,1,0:T(8,128)} fusion(f32[64,16,16]{2,1,0:T(8,128)S(1)} %get-tuple-element.653, s32[1024]{0:T(1024)S(1)} %get-tuple-element.622), kind=kCustom, calls=%fused_computation.clone.clone.1 | custom fusion | bytes 2101248 | tf_op jit(solution)/shard_map/while/body/eval_jaxpr/while/body/eval_jaxpr/jit(_take)/gather | solution.py:56
  131.9 10.4 %fusion.78 = bf16[1024,16,16]{2,1,0:T(8,128)(2,1)} fusion(bf16[1024,16,16]{2,1,0:T(8,128)(2,1)} %copy.28, f32[1024,16,16]{2,1,0:T(8,128)} %gather_fusion.3, pred[1024]{0:T(1024)(128)(4,1)S(1)} %compare_and_fusion.7), kind=kOutput, calls=%fused_computation.36.clone.1 | convolution fusion | flops 50855936 | bytes 2098176 | tf_op jit(solution)/shard_map/while/body/eval_jaxpr/while/body/eval_jaxpr/eij,ejc->eic/dot_general | solution.py:57
  142.3 4.4 %copy.29 = bf16[1024,16,16]{0,2,1:T(8,128)(2,1)S(1)} copy(bf16[1024,16,16]{2,1,0:T(8,128)(2,1)} %fusion.78) | data formatting | bytes 1048576 | tf_op jit(solution)/shard_map/while/body/eval_jaxpr/while/body/eval_jaxpr/convert_element_type | solution.py:60
  146.7 11.9 %fusion.79 = f32[8192,256]{1,0:T(8,128)} fusion(bf16[1024,256]{0,1:T(8,128)(2,1)S(1)} %bitcast.42, s32[1024]{0:T(1024)S(1)} %dynamic_slice.97, pred[1024]{0:T(1024)(128)(4,1)S(1)} %get-tuple-element.623, f32[8192,256]{1,0:T(8,128)} %get-tuple-element.637, pred[]{:T(512)S(6)} %compare.3), kind=kOutput, calls=%fused_computation.31.clone.1 | convolution fusion | flops 4315938816 | bytes 17306624 | tf_op jit(solution)/shard_map/while/body/eval_jaxpr/while/body/eval_jaxpr/dot_general | solution.py:65
  158.6 98.5 %while.44 = (s32[]{:T(128)}, f32[8192,256]{1,0:T(8,128)}, s32[2048]{0:T(1024)S(1)}, s32[]{:T(128)}, s32[2048]{0:T(1024)S(1)}, /*index=5*/f32[64,16,16]{2,1,0:T(8...) while((s32[]{:T(128)}, f32[8192,256]{1,0:T(8,128)}, ...), condition=%wide.region_3.0_spmd.clone, body=%wide.region_2.5_spmd.clone.sunk | while | flops 4364982272 | bytes 26790076 | solution.py:68
  159.3 6.2 %gather_fusion = bf16[1024,256]{1,0:T(8,128)(2,1)S(1)} fusion(bf16[8192,256]{1,0:T(8,128)(2,1)} %get-tuple-element.691, s32[1024]{0:T(1024)S(1)} %get-tuple-element.608), kind=kCustom, calls=%fused_computation.3.clone.clone.1 | custom fusion | bytes 1052672 | tf_op jit(solution)/shard_map/while/body/eval_jaxpr/while/body/eval_jaxpr/jit(_take)/gather | solution.py:52
  165.9 4.7 %copy.25 = bf16[1024,16,16]{2,1,0:T(8,128)(2,1)} copy(bf16[1024,16,16]{0,2,1:T(8,128)(2,1)S(1)} %bitcast.41) | data formatting | bytes 1048576 | tf_op jit(solution)/shard_map/while/body/eval_jaxpr/while/body/eval_jaxpr/reshape | solution.py:54
  170.7 10.6 %gather_fusion.1 = f32[1024,16,16]{2,1,0:T(8,128)} fusion(f32[64,16,16]{2,1,0:T(8,128)S(1)} %get-tuple-element.689, s32[1024]{0:T(1024)S(1)} %get-tuple-element.610), kind=kCustom, calls=%fused_computation.2.clone.clone.1 | custom fusion | bytes 2101248 | tf_op jit(solution)/shard_map/while/body/eval_jaxpr/while/body/eval_jaxpr/jit(_take)/gather | solution.py:56
  181.3 10.4 %fusion.71 = bf16[1024,16,16]{2,1,0:T(8,128)(2,1)} fusion(bf16[1024,16,16]{2,1,0:T(8,128)(2,1)} %copy.25, f32[1024,16,16]{2,1,0:T(8,128)} %gather_fusion.1, pred[1024]{0:T(1024)(128)(4,1)S(1)} %compare_and_fusion.6), kind=kOutput, calls=%fused_computation.16.clone.1 | convolution fusion | flops 50855936 | bytes 2098176 | tf_op jit(solution)/shard_map/while/body/eval_jaxpr/while/body/eval_jaxpr/eij,ejc->eic/dot_general | solution.py:57
  191.7 4.4 %copy.26 = bf16[1024,16,16]{0,2,1:T(8,128)(2,1)S(1)} copy(bf16[1024,16,16]{2,1,0:T(8,128)(2,1)} %fusion.71) | data formatting | bytes 1048576 | tf_op jit(solution)/shard_map/while/body/eval_jaxpr/while/body/eval_jaxpr/convert_element_type | solution.py:60
  196.2 11.8 %fusion.72 = f32[8192,256]{1,0:T(8,128)} fusion(f32[8192,256]{1,0:T(8,128)} %get-tuple-element.673, bf16[1024,256]{0,1:T(8,128)(2,1)S(1)} %bitcast.43, s32[1024]{0:T(1024)S(1)} %dynamic_slice.94, pred[1024]{0:T(1024)(128)(4,1)S(1)} %get-tuple-element.611), kind=kOutput, calls=%fused_computation.11.clone.1 | convolution fusion | flops 4313841664 | bytes 17306624 | tf_op jit(solution)/shard_map/while/body/eval_jaxpr/while/body/eval_jaxpr/dot_general | solution.py:65
  208.6 6.2 %gather_fusion = bf16[1024,256]{1,0:T(8,128)(2,1)S(1)} fusion(bf16[8192,256]{1,0:T(8,128)(2,1)} %get-tuple-element.691, s32[1024]{0:T(1024)S(1)} %get-tuple-element.608), kind=kCustom, calls=%fused_computation.3.clone.clone.1 | custom fusion | bytes 1052672 | tf_op jit(solution)/shard_map/while/body/eval_jaxpr/while/body/eval_jaxpr/jit(_take)/gather | solution.py:52
  215.2 4.7 %copy.25 = bf16[1024,16,16]{2,1,0:T(8,128)(2,1)} copy(bf16[1024,16,16]{0,2,1:T(8,128)(2,1)S(1)} %bitcast.41) | data formatting | bytes 1048576 | tf_op jit(solution)/shard_map/while/body/eval_jaxpr/while/body/eval_jaxpr/reshape | solution.py:54
  220.0 10.6 %gather_fusion.1 = f32[1024,16,16]{2,1,0:T(8,128)} fusion(f32[64,16,16]{2,1,0:T(8,128)S(1)} %get-tuple-element.689, s32[1024]{0:T(1024)S(1)} %get-tuple-element.610), kind=kCustom, calls=%fused_computation.2.clone.clone.1 | custom fusion | bytes 2101248 | tf_op jit(solution)/shard_map/while/body/eval_jaxpr/while/body/eval_jaxpr/jit(_take)/gather | solution.py:56
  230.6 10.4 %fusion.71 = bf16[1024,16,16]{2,1,0:T(8,128)(2,1)} fusion(bf16[1024,16,16]{2,1,0:T(8,128)(2,1)} %copy.25, f32[1024,16,16]{2,1,0:T(8,128)} %gather_fusion.1, pred[1024]{0:T(1024)(128)(4,1)S(1)} %compare_and_fusion.6), kind=kOutput, calls=%fused_computation.16.clone.1 | convolution fusion | flops 50855936 | bytes 2098176 | tf_op jit(solution)/shard_map/while/body/eval_jaxpr/while/body/eval_jaxpr/eij,ejc->eic/dot_general | solution.py:57
  241.0 4.4 %copy.26 = bf16[1024,16,16]{0,2,1:T(8,128)(2,1)S(1)} copy(bf16[1024,16,16]{2,1,0:T(8,128)(2,1)} %fusion.71) | data formatting | bytes 1048576 | tf_op jit(solution)/shard_map/while/body/eval_jaxpr/while/body/eval_jaxpr/convert_element_type | solution.py:60
  245.4 11.8 %fusion.72 = f32[8192,256]{1,0:T(8,128)} fusion(f32[8192,256]{1,0:T(8,128)} %get-tuple-element.673, bf16[1024,256]{0,1:T(8,128)(2,1)S(1)} %bitcast.43, s32[1024]{0:T(1024)S(1)} %dynamic_slice.94, pred[1024]{0:T(1024)(128)(4,1)S(1)} %get-tuple-element.611), kind=kOutput, calls=%fused_computation.11.clone.1 | convolution fusion | flops 4313841664 | bytes 17306624 | tf_op jit(solution)/shard_map/while/body/eval_jaxpr/while/body/eval_jaxpr/dot_general | solution.py:65
  259.0 76.6 %reduce-scatter.2.cloned.1.call-done = f32[2048,256]{1,0:T(8,128)} async-done(((f32[8192,256]{1,0:T(8,128)}), f32[2048,256]{1,0:T(8,128)}) %reduce-scatter.2.cloned.1.call-update) | async-done | bytes 2097168 | tf_op jit(solution)/shard_map/reduce_scatter | solution.py:71
  335.6 4.6 %fusion.40 = bf16[2048,256]{1,0:T(8,128)(2,1)} fusion(f32[2048,256]{1,0:T(8,128)} %reduce-scatter.2.cloned.1.call-done, f32[256,256]{1,0:T(8,128)S(1)} %mul.41, bf16[2048,256]{1,0:T(8,128)(2,1)} %param.15), kind=kOutput, calls=%fused_computation.47 | convolution fusion | flops 1612185600 | bytes 4456448 | tf_op jit(solution)/shard_map/dot_general | solution.py:73
  (38 shorter events, 9.4 us)
Async XLA Ops:
  6.5 52.7 %all-gather.2.cloned.1.call-start = ((), (), s32[]{:S(2)}) async-start(), calls=%async_computation.1 | async-start | bytes 5242880 | tf_op jit(solution)/shard_map/all_gather | solution.py:28
  7.3 328.3 %reduce-scatter.2.cloned.1.call-start = ((), (), s32[]{:S(2)}) async-start(), calls=%async_computation.2 | async-start | bytes 10485760 | tf_op jit(solution)/shard_map/reduce_scatter | solution.py:71
  59.2 99.4 %collective-permute-start = (bf16[8192,256]{1,0:T(8,128)(2,1)}, bf16[8192,256]{1,0:T(8,128)(2,1)}, u32[]{:S(2)}, u32[]{:S(2)}) collective-permute-start(bf16[8192,256]{1,0:T(8,128)(2,1)} %all-gather.2.cloned.1.call-done), channel_id=1, source_target_pairs={{31,0},{0,1},{1,2},{2,3},{3,4},{4,5},{5,6},{6,7},{7,8},{8,9},{9,10... | collective-permute-start | bytes 12582920 | tf_op jit(solution)/shard_map/ppermute | solution.py:10
  257.2 0.7 copy-start
Sparse Core Ops, SparseCore 0:
  9.0 50.1 all-gather.1
  257.3 78.2 reduce-scatter.1
where the time goes:
time: 348 us; the launch traced here: 347 us
  waiting for transfers between devices  124 us (36%)
  local copies, waits for them, and re-layouts  111 us (32%)
  matrix products  91.5 us (26%)
  between operations  13.4 us (4%)
  other arithmetic  3.8 us (1%)
    reduce_scatter x1, waiting for transfers between devices, body(): lax.psum_scatter(partial_value, 'rep', scatter_dimension=0, tiled=True)  76.6 us
    all_gather x1, waiting for transfers between devices, body(): source_block = lax.all_gather(features, 'rep', axis=0, tiled=True)  46.9 us
    dot_general x4, matrix products, add_block(): jnp.dot(selector, message, preferred_element_type=jnp.float32)  45.3 us
    gather x4, local copies, waits for them, and re-layouts, add_block(): chosen = jnp.take(restriction, map_part, axis=0)  42.5 us
    dot_general x4, matrix products, add_block(): jnp.einsum('eij,ejc->eic', chosen, gathered, precision=lax.Precision.HIGH...  41.6 us
    gather x4, local copies, waits for them, and re-layouts, add_block(): jnp.take(source_block, source_part, axis=0).astype(jnp.float32)  24.8 us
    reshape x4, local copies, waits for them, and re-layouts, add_block(): gathered = jnp.take(source_block, source_part, axis=0).astype(jnp.float32...  19 us
    convert_element_type x4, local copies, waits for them, and re-layouts, add_block(): message = message.reshape(edge_block, feature_width).astype(jnp.bfloat16)  17.6 us
  transfers between devices with their start and end apart: 3, of which 2 were waited for; matrix products, arithmetic and copies ran while one was open for 30% of the time, Pallas kernels for 0%

commit v1 on v0

v1 whole, which is shorter than its diff:
```python
import functools

import jax
import jax.numpy as jnp
from jax import lax
from jax.experimental import pallas as pl
from jax.experimental.pallas import tpu as pltpu
from jax.sharding import PartitionSpec as P

MESH = pl.DeviceIdType.MESH
PIECES = 4
SLOTS = 256
GROUP = 16
ACCS = 2


def exchange_kernel(dims, features, index_ref, restriction_ref, own, prev, list_ref, count_ref, bank_ref,
                    indices, packed, position, index_send, index_recv, send, recv):
    reps, blocks, rows, stalk, channels = dims
    rep = lax.axis_index("rep")
    blk = lax.axis_index("blk")
    pair = lax.rem(rep + 2, 4)
    mate = rep + 1 - 2 * lax.rem(rep, 2)
    far = lax.rem(mate + 2, 4)
    after = lax.rem(blk + 1, blocks)
    before = lax.rem(blk + blocks - 1, blocks)
    to_mate = {"rep": mate, "blk": blk}
    to_pair = {"rep": pair, "blk": blk}
    to_far = {"rep": far, "blk": blk}
    to_next = {"rep": pair, "blk": after}
    from_last = {"rep": pair, "blk": before}

    barrier = pltpu.get_barrier_semaphore()
    for other in (to_mate, to_pair, to_far, to_next, from_last):
        pl.semaphore_signal(barrier, inc=1, device_id=other, device_id_type=MESH)
    pl.semaphore_wait(barrier, 5)

    def index_copy(k, other):
        return pltpu.make_async_remote_copy(
            src_ref=index_ref, dst_ref=indices.at[rep], send_sem=index_send.at[k], recv_sem=index_recv.at[k],
            device_id=other, device_id_type=MESH)

    index_copies = [index_copy(k, other) for k, other in enumerate((to_mate, to_pair, to_far))]
    for copy in index_copies:
        copy.start()

    piece = rows // PIECES

    def rows_of(k):
        return pl.ds(k * piece, piece)

    def remote(family, k, src, dst, other):
        return pltpu.make_async_remote_copy(
            src_ref=src, dst_ref=dst, send_sem=send.at[family, k], recv_sem=recv.at[family, k],
            device_id=other, device_id_type=MESH)

    every = range(PIECES)
    first, second = range(PIECES // 2), range(PIECES // 2, PIECES)
    to_mate_own = [remote(0, k, features.at[rows_of(k), :], own.at[rep, rows_of(k), :], to_mate) for k in every]
    to_pair_own = [remote(1, k, features.at[rows_of(k), :], own.at[rep, rows_of(k), :], to_pair) for k in every]
    to_next_own = [remote(2, k, features.at[rows_of(k), :], prev.at[rep, rows_of(k), :], to_next) for k in every]
    mate_pairs = [remote(3, k, own.at[pair, rows_of(k), :], own.at[pair, rows_of(k), :], to_mate) for k in every]
    mate_lasts = [remote(4, k, prev.at[pair, rows_of(k), :], prev.at[pair, rows_of(k), :], to_mate) for k in every]
    next_pairs = [remote(5, k, own.at[pair, rows_of(k), :], prev.at[pair, rows_of(k), :], to_next) for k in first]
    pair_lasts = [remote(6, k - PIECES // 2, prev.at[pair, rows_of(k), :], prev.at[pair, rows_of(k), :], to_pair) for k in second]
    mate_rest = [remote(7, k, prev.at[rep, rows_of(k), :], prev.at[rep, rows_of(k), :], to_mate) for k in every]

    for k in every:
        to_pair_own[k].start()
        to_next_own[k].start()
        to_mate_own[k].start()

    indices[rep] = index_ref[...]
    for copy in index_copies:
        copy.wait_recv()
    per_rep = index_ref.shape[1]
    chunks = reps * per_rep
    sources = indices[:, 0].reshape(chunks, SLOTS)
    targets = indices[:, 1].reshape(chunks, SLOTS)
    maps = indices[:, 2].reshape(chunks, SLOTS)
    here = (targets // rows) == rep
    earlier = (lax.broadcasted_iota(jnp.int32, (SLOTS, SLOTS), 0) <= lax.broadcasted_iota(jnp.int32, (SLOTS, SLOTS), 1))
    running = jnp.dot(
        here.astype(jnp.float32).astype(jnp.bfloat16), earlier.astype(jnp.float32).astype(jnp.bfloat16),
        preferred_element_type=jnp.float32).astype(jnp.int32)
    count_ref[...] = running[:, SLOTS - 128:]
    position[...] = jnp.where(here, running - 1, -1)
    packed[...] = sources + (targets & (rows - 1)) * 8192 + maps * (8192 * 4096)
    shift = 8 * jnp.minimum(lax.broadcasted_iota(jnp.int32, (8, SLOTS), 0), 3)
    used = lax.broadcasted_iota(jnp.int32, (8, SLOTS), 0) < 4
    place = lax.broadcasted_iota(jnp.int32, (SLOTS, SLOTS), 0)
    slot = lax.broadcasted_iota(jnp.int32, (8, SLOTS), 1)

    def compress(c, carry):
        at = position[pl.ds(c, 1), :]
        word = jnp.broadcast_to(packed[pl.ds(c, 1), :], (8, SLOTS))
        digits = (lax.shift_right_logical(word, shift) & 255).astype(jnp.float32).astype(jnp.bfloat16)
        chosen = jnp.where(place == at, 1.0, 0.0).astype(jnp.bfloat16)
        moved = lax.dot_general(digits, chosen, (((1,), (1,)), ((), ())), preferred_element_type=jnp.float32)
        whole = jnp.where(used, moved.astype(jnp.int32) << shift, 0)
        whole = jnp.sum(whole, axis=0, keepdims=True)
        total = jnp.max(jnp.broadcast_to(at, (8, SLOTS)), axis=1, keepdims=True) + 1
        list_ref[pl.ds(c, 1), :] = jnp.where(slot < total, jnp.broadcast_to(whole, (8, SLOTS)), rows * 8192)[0:1]
        return carry

    lax.fori_loop(0, chunks, compress, 0)

    width = stalk * channels
    bank = restriction_ref[...]
    high = bank.astype(jnp.bfloat16)
    left = bank - high.astype(jnp.float32)
    middle = left.astype(jnp.bfloat16)
    low = (left - middle.astype(jnp.float32)).astype(jnp.bfloat16)
    row_of = lax.broadcasted_iota(jnp.int32, (stalk * stalk, width), 0)
    lane_of = lax.broadcasted_iota(jnp.int32, (stalk * stalk, width), 1) // channels
    for s in range(stalk):
        wanted = lane_of * stalk + ((lane_of - s) & (stalk - 1))
        pick = jnp.where(row_of == wanted, 1.0, 0.0).astype(jnp.bfloat16)
        spread = jnp.dot(high, pick, preferred_element_type=jnp.float32)
        spread = spread + jnp.dot(middle, pick, preferred_element_type=jnp.float32)
        spread = spread + jnp.dot(low, pick, preferred_element_type=jnp.float32)
        bank_ref[:, s, :] = spread

    for k in every:
        to_pair_own[k].wait_recv()
        mate_pairs[k].start()
        if k in first:
            next_pairs[k].start()
        to_next_own[k].wait_recv()
        mate_lasts[k].start()
        if k in second:
            pair_lasts[k - PIECES // 2].start()
    for k in first:
        next_pairs[k].wait_recv()
        mate_rest[k].start()
        pair_lasts[k].wait_recv()
        mate_rest[k + PIECES // 2].start()
    for family in (to_mate_own, mate_pairs, mate_lasts, mate_rest):
        for copy in family:
            copy.wait_recv()
    for copy in index_copies:
        copy.wait_send()
    for family in (to_mate_own, to_pair_own, to_next_own, mate_pairs, mate_lasts, next_pairs, pair_lasts, mate_rest):
        for copy in family:
            copy.wait_send()


def exchange(dims, features, indices, restriction):
    reps, blocks, rows, stalk, channels = dims
    width = stalk * channels
    chunks = reps * indices.shape[1]
    anywhere = pl.BlockSpec(memory_space=pl.ANY)
    vmem = pl.BlockSpec(memory_space=pltpu.VMEM)
    block = jax.ShapeDtypeStruct((reps, rows, width), features.dtype)
    return pl.pallas_call(
        functools.partial(exchange_kernel, dims),
        out_shape=(
            block,
            block,
            jax.ShapeDtypeStruct((chunks, SLOTS), jnp.int32),
            jax.ShapeDtypeStruct((chunks, 128), jnp.int32),
            jax.ShapeDtypeStruct((restriction.shape[0], stalk, width), jnp.float32),
        ),
        in_specs=[anywhere, vmem, vmem],
        out_specs=(anywhere, anywhere, vmem, vmem, vmem),
        scratch_shapes=[
            pltpu.VMEM((reps, *indices.shape), jnp.int32),
            pltpu.VMEM((chunks, SLOTS), jnp.int32),
            pltpu.VMEM((chunks, SLOTS), jnp.int32),
            pltpu.SemaphoreType.DMA((3,)),
            pltpu.SemaphoreType.DMA((3,)),
            pltpu.SemaphoreType.DMA((8, PIECES)),
            pltpu.SemaphoreType.DMA((8, PIECES)),
        ],
        compiler_params=pltpu.CompilerParams(collective_id=0, has_side_effects=True, vmem_limit_bytes=24 << 20),
        name="exchange",
    )(features, indices, restriction)


def column_sums(parts, sub):
    step = 1
    while len(parts) > 1:
        keep = (sub & step) == 0
        half = len(parts) // 2
        joined = []
        for a, b in zip(parts[:half], parts[half:]):
            joined.append(jnp.where(keep, a, b) + pltpu.roll(jnp.where(keep, b, a), step, 0))
        parts = joined
        step *= 2
    return parts[0]


def edge_kernel(dims, feat_ref, own_ref, prev_ref, me_ref, list_ref, count_ref, bank_ref, spread_ref, out_ref,
                stage, table, ring, *rest):
    reps, rows, width, steps, chunks, slots = dims
    accs, (sems,) = rest[:ACCS], rest[ACCS:]
    half = width // 2
    me = me_ref[0]
    def fetch(turn, shard, start):
        dst = stage.at[turn, shard]
        sem = sems.at[turn, shard]
        if turn == 0:
            @pl.when(shard == me)
            def _():
                c = pltpu.make_async_copy(feat_ref, dst, sem)
                c.start() if start else c.wait()
            @pl.when(shard != me)
            def _():
                c = pltpu.make_async_copy(own_ref.at[shard], dst, sem)
                c.start() if start else c.wait()
        else:
            c = pltpu.make_async_copy(prev_ref.at[shard], dst, sem)
            c.start() if start else c.wait()
    for turn in range(steps):
        for shard in range(reps):
            fetch(turn, shard, True)
    def clear(i, _):
        at = pl.ds(pl.multiple_of(i * 128, 128), 128)
        for a in accs:
            a[at, :] = jnp.zeros((128, half), jnp.float32)
        return 0
    lax.fori_loop(0, accs[0].shape[0] // 128, clear, 0)
    lane = lax.broadcasted_iota(jnp.int32, (8, half), 1)
    sub = lax.broadcasted_iota(jnp.int32, (8, half), 0)
    straight = lane >= sub * 16
    for turn in range(steps):
        for shard in range(reps):
            fetch(turn, shard, False)
            def widen(i, _, shard=shard, turn=turn):
                src = pl.ds(pl.multiple_of(i * 128, 128), 128)
                dst = pl.ds(pl.multiple_of(shard * rows + i * 128, 128), 128)
                wide = stage[turn, shard, src, :].astype(jnp.float32)
                table[dst, :] = wide[:, 0:half]
                table[pl.ds(pl.multiple_of((reps + shard) * rows + i * 128, 128), 128), :] = wide[:, half:width]
                return 0
            lax.fori_loop(0, rows // 128, widen, 0)
        def chunk(c, _, turn=turn):
            per = chunks // (reps * steps)
            at = (c // per) * (per * steps) + turn * per + c % per
            n = count_ref[at]
            def group(g, _):
                first = at * slots + g * GROUP
                for base in range(0, GROUP, 8):
                    lows, highs, targets = [], [], []
                    for u in range(8):
                        p = list_ref[first + base + u]
                        src = p & 8191
                        targets.append((p >> 12) & 8190)
                        m = p >> 25
                        a = pltpu.roll(table[pl.ds(src, 8, stride=0), :], 0, 1, stride=16, stride_axis=0)
                        b = pltpu.roll(table[pl.ds(src + reps * rows, 8, stride=0), :], 0, 1, stride=16, stride_axis=0)
                        glo = jnp.where(straight, a, b)
                        ghi = jnp.where(straight, b, a)
                        lows.append(bank_ref[m, 0:8, 0:half] * glo + bank_ref[m, 8:16, 0:half] * ghi)
                        highs.append(bank_ref[m, 0:8, half:width] * ghi + bank_ref[m, 8:16, half:width] * glo)
                    order = (0, 4, 2, 6, 1, 5, 3, 7)
                    for k, parts in enumerate((lows, highs)):
                        message = column_sums([parts[i] for i in order], sub)
                        ring[pl.ds(2 * base + k, 8, stride=2), :] = message.astype(jnp.bfloat16).astype(jnp.float32)
                    for u in range(8):
                        acc = accs[u % ACCS]
                        acc[pl.ds(targets[u], 2), :] += ring[pl.ds(2 * (base + u), 2), :]
                return 0
            lax.fori_loop(0, (n + GROUP - 1) // GROUP, group, 0)
            return 0
        lax.fori_loop(0, chunks // steps, chunk, 0)
    spread = spread_ref[...]
    near = spread.astype(jnp.bfloat16)
    rest_ = (spread - near.astype(jnp.float32)).astype(jnp.bfloat16)
    def finish(i, _):
        at = pl.ds(pl.multiple_of(i * 128, 128), 128)
        sides = []
        for k in range(2):
            where = pl.ds(pl.multiple_of(i * 256, 256) + k, 128, stride=2)
            side = accs[0][where, :]
            for a in accs[1:]:
                side = side + a[where, :]
            sides.append(side)
        total = jnp.concatenate(sides, axis=1)
        top = total.astype(jnp.bfloat16)
        low = (total - top.astype(jnp.float32)).astype(jnp.bfloat16)
        mixed = jnp.dot(top, near, preferred_element_type=jnp.float32)
        mixed = mixed + jnp.dot(low, near, preferred_element_type=jnp.float32)
        mixed = mixed + jnp.dot(top, rest_, preferred_element_type=jnp.float32)
        own = stage[0, me, at, :].astype(jnp.float32)
        out_ref[at, :] = (own + mixed).astype(jnp.bfloat16)
        return 0
    lax.fori_loop(0, rows // 128, finish, 0)


def edges(feat, own, prev, me, lists, counts, bank, spread):
    reps, rows, width = own.shape
    chunks = counts.shape[0]
    slots = lists.shape[0] // chunks
    dims = (reps, rows, width, 2, chunks, slots)
    any_ = pl.BlockSpec(memory_space=pl.ANY)
    smem = pl.BlockSpec(memory_space=pltpu.SMEM)
    vmem = pl.BlockSpec(memory_space=pltpu.VMEM)
    return pl.pallas_call(
        functools.partial(edge_kernel, dims),
        out_shape=jax.ShapeDtypeStruct((rows, width), jnp.bfloat16),
        in_specs=[any_, any_, any_, smem, smem, smem, vmem, vmem],
        out_specs=vmem,
        scratch_shapes=[
            pltpu.VMEM((2, reps, rows, width), jnp.bfloat16),
            pltpu.VMEM((2 * reps * rows, width // 2), jnp.float32),
            pltpu.VMEM((2 * GROUP, width // 2), jnp.float32),
            *[pltpu.VMEM((2 * rows + 128, width // 2), jnp.float32)] * ACCS,
            pltpu.SemaphoreType.DMA((2, reps)),
        ],
        compiler_params=pltpu.CompilerParams(vmem_limit_bytes=60 << 20),
    )(feat, own, prev, me, lists, counts, bank, spread)


def body(features, restriction, mixing, source_index, target_index, map_index, edge_counts):
    rows = features.shape[0]
    stalk = restriction.shape[1]
    channels = mixing.shape[0]
    steps, capacity = source_index.shape[2:]
    dims = (lax.axis_size("rep"), lax.axis_size("blk"), rows, stalk, channels)
    live = lax.broadcasted_iota(jnp.int32, (steps, capacity), 1) < edge_counts[0, 0][:, None]
    targets = jnp.where(live, target_index[0, 0], dims[0] * rows)
    indices = jnp.stack([source_index[0, 0], targets, map_index[0, 0]])
    indices = indices.reshape(3, steps * capacity // SLOTS, SLOTS)
    own, prev, lists, counts, bank = exchange(dims, features, indices, restriction.reshape(-1, stalk * stalk))
    spread = jnp.kron(jnp.eye(stalk, dtype=jnp.float32), mixing)
    me = lax.axis_index("rep").astype(jnp.int32).reshape(1)
    return edges(features, own, prev, me, lists.reshape(-1), counts[:, 127], bank, spread)


def solution(mesh):
    in_specs = (
        P(("blk", "rep"), None),
        P(),
        P(),
        P("blk", "rep", None, None),
        P("blk", "rep", None, None),
        P("blk", "rep", None, None),
        P("blk", "rep", None),
    )
    out_specs = P(("blk", "rep"), None)
    return jax.shard_map(body, mesh=mesh, in_specs=in_specs, out_specs=out_specs, check_vma=False)
```

time: 348 us -> 94.7 us (0.27)
  the two profiles are of different devices: /device:TPU:1 before, /device:TPU:75 now
where the time goes in v1:
time: 94.7 us; the launch traced here: 96.4 us
  Pallas kernels  83.5 us (88%)
  local copies, waits for them, and re-layouts  11.8 us (12%)
  other arithmetic  1 us (1%)
    pallas_call x1, Pallas kernels, edges(): pl.pallas_call(functools.partial(edge_kernel, dims), out_shape=jax.ShapeD...  42.3 us
    pallas_call x1, Pallas kernels, exchange(): pl.pallas_call(functools.partial(exchange_kernel, dims), out_shape=(block...  41.2 us
    unnamed x9, local copies, waits for them, and re-layouts  5.61 us

profile of v1, /device:TPU:75, one launch (start us, length us, event | category | flops | bytes accessed | tf_op | source)
XLA Modules:
  0.0 96.4 jit_solution(7196088258920049953)
XLA Ops:
  0.0 0.7 stack.8
  0.7 0.7 squeeze.6
  1.5 0.7 stack.9
  2.2 0.7 lt.21
  3.0 1.0 %copy.9.restriction_ref = f32[64,256]{1,0:T(8,128)S(1)} copy(f32[64,256]{0,1:T(8,128)} %bitcast.11) | data formatting | bytes 131072 | tf_op jit(solution)/shard_map/reshape | solution.py:325
  4.0 0.0 copy-start.2
  4.0 1.0 %broadcast_multiply_fusion = f32[16,16,16,16]{3,2,1,0:T(8,128)S(1)} fusion(f32[16,16]{1,0:T(8,128)} %param.9, f32[16,16]{1,0:T(8,128)S(1)} %fusion), kind=kLoop, calls=%fused_computation | loop fusion | flops 65536 | bytes 264192 | tf_op jit(solution)/shard_map/jit(kron)/mul | solution.py:326
  5.0 1.5 %mul.27.spread_ref = f32[256,256]{1,0:T(8,128)} reshape(f32[16,16,16,16]{3,2,1,0:T(8,128)S(1)} %broadcast_multiply_fusion) | data formatting | bytes 524288 | tf_op jit(solution)/shard_map/jit(kron)/mul | solution.py:326
  6.6 0.0 copy-done.2
  6.6 41.2 %exchange.1 = (bf16[4,2048,256]{2,1,0:T(8,128)(2,1)S(1)}, bf16[4,2048,256]{2,1,0:T(8,128)(2,1)S(1)}, s32[64,256]{1,0:T(8,128)S(1)}, s32[64,128]{1,0:T(8,128)S(1)}, f32[64,16,256]{2,1,0:T(8,128)S(1)}) custom-call(bf16[2048,256]{1,0:T(8,128)(2,1)S(1)} %copy-done.2, s32[3,16,256]{2,1,0:T(8,128)S(1)} %pad_add_fusion.index_ref, f32[64,256]{1,0:T(8,128)S(1)} %copy.9.restriction_ref), custom_call_target="tpu_custom_call" | custom-call | tf_op jit(solution)/shard_map/exchange/pallas_call | solution.py:155
  47.7 0.0 copy-start
  47.8 1.9 %copy-done = bf16[4,2048,256]{2,1,0:T(8,128)(2,1)} copy-done((bf16[4,2048,256]{2,1,0:T(8,128)(2,1)}, bf16[4,2048,256]{2,1,0:T(8,128)(2,1)S(1)}, u32[]{:S(2)}) %copy-start) | copy-done | bytes 4194328
  49.7 0.0 copy-start.1
  49.7 2.0 %copy-done.1 = bf16[4,2048,256]{2,1,0:T(8,128)(2,1)} copy-done((bf16[4,2048,256]{2,1,0:T(8,128)(2,1)}, bf16[4,2048,256]{2,1,0:T(8,128)(2,1)S(1)}, u32[]{:S(2)}) %copy-start.1) | copy-done | bytes 4194328
  51.7 0.0 copy-start.3
  51.7 1.1 %copy-done.3 = f32[64,16,256]{2,1,0:T(8,128)} copy-done((f32[64,16,256]{2,1,0:T(8,128)}, f32[64,16,256]{2,1,0:T(8,128)S(1)}, u32[]{:S(2)}) %copy-start.3) | copy-done | bytes 1048600
  52.7 0.7 slice_reduce_fusion.count_ref
  53.4 0.6 copy.10
  54.1 42.3 %shard_map.73 = bf16[2048,256]{1,0:T(8,128)(2,1)} custom-call(bf16[2048,256]{1,0:T(8,128)(2,1)} %feat_ref.1, bf16[4,2048,256]{2,1,0:T(8,128)(2,1)} %copy-done, bf16[4,2048,256]{2,1,0:T(8,128)(2,1)} %copy-done.1, s32[1]{0:T(128)} %bitcast.2.me_ref, s32[16384]{0:T(1024)} %bitcast.10, s32[64]{0:T(128)} %slice_reduce_fusion.count_ref, f32[64,16,256]{2,1,0:T(8,128)} %copy-done.3, ...), custom_call_target="tpu_custom_call" | custom-call | tf_op jit(solution)/shard_map/pallas_call | solution.py:299
  (6 shorter events, 0.1 us)
Async XLA Ops:
  4.0 2.5 %copy-start.2 = (bf16[2048,256]{1,0:T(8,128)(2,1)S(1)}, bf16[2048,256]{1,0:T(8,128)(2,1)}, u32[]{:S(2)}) copy-start(bf16[2048,256]{1,0:T(8,128)(2,1)} %feat_ref.1) | copy-start | bytes 3145732
  47.7 1.9 %copy-start = (bf16[4,2048,256]{2,1,0:T(8,128)(2,1)}, bf16[4,2048,256]{2,1,0:T(8,128)(2,1)S(1)}, u32[]{:S(2)}) copy-start(bf16[4,2048,256]{2,1,0:T(8,128)(2,1)S(1)} %get-tuple-element.10.own_ref) | copy-start | bytes 12582916
  49.7 2.0 %copy-start.1 = (bf16[4,2048,256]{2,1,0:T(8,128)(2,1)}, bf16[4,2048,256]{2,1,0:T(8,128)(2,1)S(1)}, u32[]{:S(2)}) copy-start(bf16[4,2048,256]{2,1,0:T(8,128)(2,1)S(1)} %get-tuple-element.11.prev_ref) | copy-start | bytes 12582916
  51.7 1.1 %copy-start.3 = (f32[64,16,256]{2,1,0:T(8,128)}, f32[64,16,256]{2,1,0:T(8,128)S(1)}, u32[]{:S(2)}) copy-start(f32[64,16,256]{2,1,0:T(8,128)S(1)} %get-tuple-element.14.bank_ref) | copy-start | bytes 3145732

commit v2 on v1

v2 whole, which is shorter than its diff:
```python
import functools

import jax
import jax.numpy as jnp
from jax import lax
from jax.experimental import pallas as pl
from jax.experimental.pallas import tpu as pltpu
from jax.sharding import PartitionSpec as P

MESH = pl.DeviceIdType.MESH
PIECES = 4
SLOTS = 256
BLOCK = 8192
GROUP = 16
EIGHTS = GROUP // 8
ACCS = 4


def exchange_kernel(dims, features, source_ref, target_ref, map_ref, count_ref, restriction_ref, mixing_ref,
                    own, prev, list_ref, live_ref, bank_ref, spread_ref,
                    sources, targets, maps, counts, packed, position, home_sem, index_send, index_recv, send, recv):
    reps, blocks, rows, stalk, channels = dims
    width = stalk * channels
    half = width // 2
    rep = lax.axis_index("rep")
    blk = lax.axis_index("blk")
    pair = lax.rem(rep + 2, 4)
    mate = rep + 1 - 2 * lax.rem(rep, 2)
    far = lax.rem(mate + 2, 4)
    after = lax.rem(blk + 1, blocks)
    before = lax.rem(blk + blocks - 1, blocks)
    to_mate = {"rep": mate, "blk": blk}
    to_pair = {"rep": pair, "blk": blk}
    to_far = {"rep": far, "blk": blk}
    to_next = {"rep": pair, "blk": after}
    from_last = {"rep": pair, "blk": before}

    barrier = pltpu.get_barrier_semaphore()
    for other in (to_mate, to_pair, to_far, to_next, from_last):
        pl.semaphore_signal(barrier, inc=1, device_id=other, device_id_type=MESH)
    pl.semaphore_wait(barrier, 5)

    home = pltpu.make_async_copy(features, own.at[rep], home_sem)
    home.start()
    index_copies = []
    for a, (src, dst) in enumerate(((source_ref, sources), (target_ref, targets), (map_ref, maps), (count_ref, counts))):
        for k, other in enumerate((to_mate, to_pair, to_far)):
            index_copies.append(pltpu.make_async_remote_copy(
                src_ref=src, dst_ref=dst.at[rep], send_sem=index_send.at[a, k], recv_sem=index_recv.at[a, k],
                device_id=other, device_id_type=MESH))
    for copy in index_copies:
        copy.start()

    piece = rows // PIECES

    def rows_of(k):
        return pl.ds(k * piece, piece)

    def remote(family, k, src, dst, other):
        return pltpu.make_async_remote_copy(
            src_ref=src, dst_ref=dst, send_sem=send.at[family, k], recv_sem=recv.at[family, k],
            device_id=other, device_id_type=MESH)

    every = range(PIECES)
    first, second = range(PIECES // 2), range(PIECES // 2, PIECES)
    to_mate_own = [remote(0, k, features.at[rows_of(k), :], own.at[rep, rows_of(k), :], to_mate) for k in every]
    to_pair_own = [remote(1, k, features.at[rows_of(k), :], own.at[rep, rows_of(k), :], to_pair) for k in every]
    to_next_own = [remote(2, k, features.at[rows_of(k), :], prev.at[rep, rows_of(k), :], to_next) for k in every]
    mate_pairs = [remote(3, k, own.at[pair, rows_of(k), :], own.at[pair, rows_of(k), :], to_mate) for k in every]
    mate_lasts = [remote(4, k, prev.at[pair, rows_of(k), :], prev.at[pair, rows_of(k), :], to_mate) for k in every]
    next_pairs = [remote(5, k, own.at[pair, rows_of(k), :], prev.at[pair, rows_of(k), :], to_next) for k in first]
    pair_lasts = [remote(6, k - PIECES // 2, prev.at[pair, rows_of(k), :], prev.at[pair, rows_of(k), :], to_pair) for k in second]
    mate_rest = [remote(7, k, prev.at[rep, rows_of(k), :], prev.at[rep, rows_of(k), :], to_mate) for k in every]

    for k in every:
        to_pair_own[k].start()
        to_next_own[k].start()
        to_mate_own[k].start()

    for src, dst in ((source_ref, sources), (target_ref, targets), (map_ref, maps), (count_ref, counts)):
        dst[rep] = src[...]
    for copy in index_copies:
        copy.wait_recv()
    steps, capacity = source_ref.shape[2:]
    runs = capacity // SLOTS
    chunks = reps * runs * steps
    spot = lax.broadcasted_iota(jnp.int32, (steps, SLOTS), 1)
    for r in range(reps):
        live = counts[r, 0]
        live = jnp.concatenate([jnp.broadcast_to(live[:, s:s + 1], (1, SLOTS)) for s in range(steps)], axis=0)
        for j in range(runs):
            part = pl.ds(j * SLOTS, SLOTS)
            to = sources.at[r, 0, 0, :, part][...]
            hit = targets.at[r, 0, 0, :, part][...]
            by = maps.at[r, 0, 0, :, part][...]
            here = (hit // rows == rep) & (spot + j * SLOTS < live)
            at = pl.ds((r * runs + j) * steps, steps)
            packed[at, :] = to + by * BLOCK + (hit & (rows - 1)) * (BLOCK * 128)
            position[at, :] = jnp.where(here, 1, 0)
    earlier = (lax.broadcasted_iota(jnp.int32, (SLOTS, SLOTS), 0) <= lax.broadcasted_iota(jnp.int32, (SLOTS, SLOTS), 1))
    here = position[...]
    running = jnp.dot(
        here.astype(jnp.float32).astype(jnp.bfloat16), earlier.astype(jnp.float32).astype(jnp.bfloat16),
        preferred_element_type=jnp.float32).astype(jnp.int32)
    live_ref[...] = running[:, SLOTS - 128:]
    position[...] = jnp.where(here > 0, running - 1, -1)
    unused = rows * (BLOCK * 128) - 2**32
    shift = 8 * jnp.minimum(lax.broadcasted_iota(jnp.int32, (8, SLOTS), 0), 3)
    used = lax.broadcasted_iota(jnp.int32, (8, SLOTS), 0) < 4
    place = lax.broadcasted_iota(jnp.int32, (SLOTS, SLOTS), 0)
    slot = lax.broadcasted_iota(jnp.int32, (8, SLOTS), 1)
    list_ref[chunks:chunks + 8, :] = jnp.full((8, SLOTS), unused, jnp.int32)

    def compress(c, carry):
        at = position[pl.ds(c, 1), :]
        word = jnp.broadcast_to(packed[pl.ds(c, 1), :], (8, SLOTS))
        digits = (lax.shift_right_logical(word, shift) & 255).astype(jnp.float32).astype(jnp.bfloat16)
        chosen = jnp.where(place == at, 1.0, 0.0).astype(jnp.bfloat16)
        moved = lax.dot_general(digits, chosen, (((1,), (1,)), ((), ())), preferred_element_type=jnp.float32)
        whole = jnp.where(used, moved.astype(jnp.int32) << shift, 0)
        whole = jnp.sum(whole, axis=0, keepdims=True)
        total = jnp.max(jnp.broadcast_to(at, (8, SLOTS)), axis=1, keepdims=True) + 1
        list_ref[pl.ds(c, 1), :] = jnp.where(slot < total, jnp.broadcast_to(whole, (8, SLOTS)), unused)[0:1]
        return carry

    lax.fori_loop(0, chunks, compress, 0)

    count = restriction_ref.shape[0]
    flat = restriction_ref[...].reshape(count * stalk, stalk)

    def three(x):
        high = x.astype(jnp.bfloat16)
        left = x - high.astype(jnp.float32)
        middle = left.astype(jnp.bfloat16)
        return high, middle, (left - middle.astype(jnp.float32)).astype(jnp.bfloat16)

    def ones(shape, test):
        return jnp.where(
            test(lax.broadcasted_iota(jnp.int32, shape, 0), lax.broadcasted_iota(jnp.int32, shape, 1)), 1.0, 0.0
        ).astype(jnp.bfloat16)

    eye = ones((stalk, stalk), lambda p, q: p == q)
    same = ones((width, width), lambda p, q: p // stalk == q // stalk)
    wide = ones((width, width), lambda p, q: (p & (stalk - 1)) == q // channels)
    flipped = [
        lax.dot_general(eye, part, (((1,), (1,)), ((), ())), preferred_element_type=jnp.float32).astype(jnp.bfloat16)
        for part in three(flat)]
    per = width // stalk
    for q in range(count // per):
        total = jnp.zeros((width, width), jnp.float32)
        for part in flipped:
            stacked = jnp.concatenate([part[:, q * width:(q + 1) * width]] * per, axis=0) * same
            total = total + jnp.dot(stacked, wide, preferred_element_type=jnp.float32)
        for m in range(per):
            for h in range(2):
                for l in range(2):
                    bank_ref[pl.ds(((q * per + m) * 4 + 2 * h + l) * 8, 8), :] = total[
                        m * stalk + 8 * h:m * stalk + 8 * h + 8, l * half:(l + 1) * half]

    tall = ones((width, channels), lambda p, q: (p & (channels - 1)) == q)
    broad = ones((channels, width), lambda p, q: p == (q & (channels - 1)))
    blocked = ones((width, width), lambda p, q: p // channels == q // channels)
    for k, part in enumerate(three(mixing_ref[...])[:2]):
        part = jnp.dot(tall, part, preferred_element_type=jnp.float32).astype(jnp.bfloat16)
        spread_ref[k] = jnp.dot(part, broad, preferred_element_type=jnp.float32).astype(jnp.bfloat16) * blocked

    for k in every:
        to_pair_own[k].wait_recv()
        mate_pairs[k].start()
        if k in first:
            next_pairs[k].start()
        to_next_own[k].wait_recv()
        mate_lasts[k].start()
        if k in second:
            pair_lasts[k - PIECES // 2].start()
    for k in first:
        next_pairs[k].wait_recv()
        mate_rest[k].start()
        pair_lasts[k].wait_recv()
        mate_rest[k + PIECES // 2].start()
    for family in (to_mate_own, mate_pairs, mate_lasts, mate_rest):
        for copy in family:
            copy.wait_recv()
    home.wait()
    for copy in index_copies:
        copy.wait_send()
    for family in (to_mate_own, to_pair_own, to_next_own, mate_pairs, mate_lasts, next_pairs, pair_lasts, mate_rest):
        for copy in family:
            copy.wait_send()


def exchange(dims, features, sources, targets, maps, counts, restriction, mixing):
    reps, blocks, rows, stalk, channels = dims
    width = stalk * channels
    chunks = reps * sources.size // SLOTS
    vmem = pl.BlockSpec(memory_space=pltpu.VMEM)
    block = jax.ShapeDtypeStruct((reps, rows, width), features.dtype)
    return pl.pallas_call(
        functools.partial(exchange_kernel, dims),
        out_shape=(
            block,
            block,
            jax.ShapeDtypeStruct((chunks + 8, SLOTS), jnp.int32),
            jax.ShapeDtypeStruct((chunks, 128), jnp.int32),
            jax.ShapeDtypeStruct((2 * restriction.shape[0] * stalk, width // 2), jnp.float32),
            jax.ShapeDtypeStruct((2, width, width), jnp.bfloat16),
        ),
        in_specs=[pl.BlockSpec(memory_space=pl.ANY)] + [vmem] * 6,
        out_specs=(vmem,) * 6,
        scratch_shapes=[
            pltpu.VMEM((reps, *sources.shape), jnp.int32),
            pltpu.VMEM((reps, *sources.shape), jnp.int32),
            pltpu.VMEM((reps, *sources.shape), jnp.int32),
            pltpu.VMEM((reps, *counts.shape), jnp.int32),
            pltpu.VMEM((chunks, SLOTS), jnp.int32),
            pltpu.VMEM((chunks, SLOTS), jnp.int32),
            pltpu.SemaphoreType.DMA,
            pltpu.SemaphoreType.DMA((4, 3)),
            pltpu.SemaphoreType.DMA((4, 3)),
            pltpu.SemaphoreType.DMA((8, PIECES)),
            pltpu.SemaphoreType.DMA((8, PIECES)),
        ],
        compiler_params=pltpu.CompilerParams(collective_id=0, has_side_effects=True, vmem_limit_bytes=28 << 20),
        name="exchange",
    )(features, sources, targets, maps, counts, restriction, mixing)


def column_sums(parts, sub):
    step = 1
    while len(parts) > 1:
        keep = (sub & step) == 0
        half = len(parts) // 2
        joined = []
        for a, b in zip(parts[:half], parts[half:]):
            joined.append(jnp.where(keep, a, b) + pltpu.roll(jnp.where(keep, b, a), step, 0))
        parts = joined
        step *= 2
    return parts[0]


def edge_kernel(dims, own_ref, prev_ref, list_ref, count_ref, bank_ref, spread_ref, out_ref,
                table, ring_even, ring_odd, starts, *rest):
    reps, rows, width, steps, chunks, slots = dims
    accs = rest
    half = width // 2
    rings = (ring_even, ring_odd)
    me = lax.axis_index("rep")
    def clear(i, _):
        at = pl.ds(pl.multiple_of(i * 128, 128), 128)
        for a in accs:
            a[at, :] = jnp.zeros((128, half), jnp.float32)
        return 0
    lax.fori_loop(0, accs[0].shape[0] // 128, clear, 0)
    sub = lax.broadcasted_iota(jnp.int32, (8, half), 0)
    diagonal = jnp.where(
        lax.broadcasted_iota(jnp.int32, (16, half), 1) // 16 == (lax.broadcasted_iota(jnp.int32, (16, half), 0) & 7), 1.0, 0.0
    ).astype(jnp.bfloat16)
    k_at = lax.broadcasted_iota(jnp.int32, (width, width), 0)
    n_at = lax.broadcasted_iota(jnp.int32, (width, width), 1)
    repeat = jnp.where((k_at % 16 == n_at % 16) & (k_at // half == n_at // half), 1.0, 0.0).astype(jnp.bfloat16)
    for turn in range(steps):
        for shard in range(reps):
            def widen(i, _, shard=shard, turn=turn):
                src = pl.ds(pl.multiple_of(i * 128, 128), 128)
                dst = pl.ds(pl.multiple_of(shard * rows + i * 128, 128), 128)
                wide = (own_ref, prev_ref)[turn][shard, src, :].astype(jnp.float32)
                table[dst, :] = wide[:, 0:half]
                table[pl.ds(pl.multiple_of((reps + shard) * rows + i * 128, 128), 128), :] = wide[:, half:width]
                return 0
            lax.fori_loop(0, rows // 128, widen, 0)
        per = chunks // (reps * steps)

        def plan(c, filled, turn=turn):
            at = c * steps + turn
            eights = (count_ref[at, 127] + 7) // 8

            def note(k, carry):
                starts[filled + k] = at * slots + 8 * k
                return carry

            lax.fori_loop(0, eights, note, 0)
            return filled + eights

        eights = lax.fori_loop(0, chunks // steps, plan, 0)
        for k in range(2 * EIGHTS):
            starts[eights + k] = chunks * slots
        groups = (eights + 2 * EIGHTS - 1) // (2 * EIGHTS)
        for k in range(2 * EIGHTS):
            starts[2 * EIGHTS * groups + k] = chunks * slots

        def words(g):
            found = []
            for k in range(EIGHTS):
                first = starts[g * EIGHTS + k]
                found += [list_ref[first + u] for u in range(8)]
            return found

        def load(now, sides, staged=None):
            for side in range(2):
                tiles = []
                for word in now[side * GROUP // 2:(side + 1) * GROUP // 2]:
                    src = word & 8191
                    both = jnp.concatenate(
                        [table[pl.ds(src, 8, stride=0), :], table[pl.ds(src + reps * rows, 8, stride=0), :]], axis=0)
                    tiles.append(both.astype(jnp.bfloat16) * diagonal)
                pairs = [jnp.concatenate(tiles[u:u + 2], axis=1) for u in range(0, GROUP // 2, 2)]
                pltpu.matmul_acc_lhs(sides[side], jnp.concatenate(pairs, axis=0), load_staged_rhs=staged)

        def add_up(now, popped, ring):
            for side in range(2):
                repeated = popped[side]
                for base in range(side * GROUP // 2, (side + 1) * GROUP // 2, 8):
                    lows, highs = [], []
                    for u in range(base, base + 8):
                        maps = bank_ref[pl.ds(pl.multiple_of((now[u] >> 8) & 2016, 32), 32), :]
                        row = u % (GROUP // 2) // 2 * 16
                        lane = u % 2 * half
                        top = repeated[row:row + 8, lane:lane + half]
                        low = repeated[row + 8:row + 16, lane:lane + half]
                        lows.append(maps[0:8] * top + maps[16:24] * low)
                        highs.append(maps[8:16] * top + maps[24:32] * low)
                    for k, parts in enumerate((lows, highs)):
                        message = column_sums([parts[i] for i in (0, 4, 2, 6, 1, 5, 3, 7)], sub)
                        ring[pl.ds(2 * base + k, 8, stride=2), :] = message.astype(jnp.bfloat16).astype(jnp.float32)
            for u in range(GROUP):
                acc = accs[u % ACCS]
                acc[pl.ds(lax.shift_right_logical(now[u], 19), 2), :] += ring[pl.ds(2 * u, 2), :]

        def run(*sides):
            even, odd = sides[:2], sides[2:]
            for side in range(2):
                pltpu.matmul_push_rhs(repeat, 0, side)
            load(words(0), even, 0)
            load(words(1), odd)

            def group(g, carry):
                for which, sides in enumerate((even, odd)):
                    popped = [pltpu.matmul_pop(side) for side in sides]
                    load(words(2 * g + which + 2), sides)
                    add_up(words(2 * g + which), popped, rings[which])
                return carry

            lax.fori_loop(0, groups, group, 0)
            for side in (*even, *odd):
                rings[0][0:8, :] = pltpu.matmul_pop(side)[0:8, 0:half]

        pl.run_scoped(run, *[pltpu.ACC(side)((4 * GROUP, width), jnp.float32) for side in (0, 1, 0, 1)])
    block = 128

    def finish(sides, i, carry):
        at = pl.ds(pl.multiple_of(i * block, block), block)
        halves = []
        for k in range(2):
            where = pl.ds(pl.multiple_of(i * 2 * block, 2 * block) + k, block, stride=2)
            side = accs[0][where, :]
            for a in accs[1:]:
                side = side + a[where, :]
            halves.append(side)
        total = jnp.concatenate(halves, axis=1)
        top = total.astype(jnp.bfloat16)
        low = (total - top.astype(jnp.float32)).astype(jnp.bfloat16)
        pltpu.matmul_acc_lhs(sides[0], top)
        pltpu.matmul_acc_lhs(sides[1], top)
        pltpu.matmul_acc_lhs(sides[0], low)
        mixed = pltpu.matmul_pop(sides[0]) + pltpu.matmul_pop(sides[1])
        own = own_ref[me, at, :].astype(jnp.float32)
        out_ref[at, :] = (own + mixed).astype(jnp.bfloat16)
        return carry

    def mix(*sides):
        blank = jnp.zeros((block, width), jnp.bfloat16)
        for side, weights in enumerate((spread_ref[0], spread_ref[1])):
            pltpu.matmul_push_rhs(weights, 0, side)
            pltpu.matmul_acc_lhs(sides[side], blank, load_staged_rhs=0)
        lax.fori_loop(0, rows // block, functools.partial(finish, sides), 0)

    pl.run_scoped(mix, *[pltpu.ACC(side)((block, width), jnp.float32) for side in range(2)])


def edges(own, prev, lists, counts, bank, spread):
    reps, rows, width = own.shape
    chunks = counts.shape[0]
    dims = (reps, rows, width, 2, chunks, SLOTS)
    smem = pl.BlockSpec(memory_space=pltpu.SMEM)
    vmem = pl.BlockSpec(memory_space=pltpu.VMEM)
    return pl.pallas_call(
        functools.partial(edge_kernel, dims),
        out_shape=jax.ShapeDtypeStruct((rows, width), own.dtype),
        in_specs=[vmem, vmem, smem, smem, vmem, vmem],
        out_specs=vmem,
        scratch_shapes=[
            pltpu.VMEM((2 * reps * rows, width // 2), jnp.float32),
            pltpu.VMEM((2 * GROUP, width // 2), jnp.float32),
            pltpu.VMEM((2 * GROUP, width // 2), jnp.float32),
            pltpu.SMEM((lists.shape[0] // 8 + 16,), jnp.int32),
            *[pltpu.VMEM((2 * rows + 128, width // 2), jnp.float32)] * ACCS,
        ],
        compiler_params=pltpu.CompilerParams(vmem_limit_bytes=36 << 20),
        name="edges",
    )(own, prev, lists, counts, bank, spread)


def body(features, restriction, mixing, source_index, target_index, map_index, edge_counts):
    rows = features.shape[0]
    stalk = restriction.shape[1]
    channels = mixing.shape[0]
    dims = (lax.axis_size("rep"), lax.axis_size("blk"), rows, stalk, channels)
    own, prev, lists, counts, bank, spread = exchange(
        dims, features, source_index, target_index, map_index, edge_counts, restriction, mixing)
    return edges(own, prev, lists.reshape(-1), counts, bank, spread)


def solution(mesh):
    in_specs = (
        P(("blk", "rep"), None),
        P(),
        P(),
        P("blk", "rep", None, None),
        P("blk", "rep", None, None),
        P("blk", "rep", None, None),
        P("blk", "rep", None),
    )
    out_specs = P(("blk", "rep"), None)
    step = jax.shard_map(body, mesh=mesh, in_specs=in_specs, out_specs=out_specs, check_vma=False)

    def run(*args):
        with jax.sharding.use_abstract_mesh(mesh.abstract_mesh):
            return step(*args)

    return run
```

time: 94.7 us -> 76 us (0.80)
  the two profiles are of different devices: /device:TPU:75 before, /device:TPU:49 now
where the time goes in v2:
time: 76 us; the launch traced here: 75.4 us
  Pallas kernels  69.4 us (91%)
  local copies, waits for them, and re-layouts  5.94 us (8%)
    pallas_call x1, Pallas kernels, exchange(): pl.pallas_call(functools.partial(exchange_kernel, dims), out_shape=(block...  45.1 us
    pallas_call x1, Pallas kernels, edges(): pl.pallas_call(functools.partial(edge_kernel, dims), out_shape=jax.ShapeD...  24.3 us
    unnamed x14, local copies, waits for them, and re-layouts  5.94 us

profile of v2, /device:TPU:49, one launch (start us, length us, event | category | flops | bytes accessed | tf_op | source)
XLA Modules:
  0.0 75.4 jit_solution(6387019566251452131)
XLA Ops:
  0.0 1.2 %copy.8.restriction_ref = f32[64,16,16]{2,1,0:T(8,128)S(1)} copy(f32[64,16,16]{0,2,1:T(8,128)} %param.8) | data formatting | bytes 131072 | tf_op args[1]
  1.2 0.0 copy-start
  1.2 1.2 %copy-done = bf16[2048,256]{1,0:T(8,128)(2,1)S(1)} copy-done((bf16[2048,256]{1,0:T(8,128)(2,1)S(1)}, bf16[2048,256]{1,0:T(8,128)(2,1)}, u32[]{:S(2)}) %copy-start) | copy-done | bytes 1048600
  2.4 0.0 copy-start.1
  2.4 0.7 copy-done.1
  3.1 0.0 copy-start.2
  3.1 0.7 copy-done.2
  3.9 0.0 copy-start.3
  3.9 0.7 copy-done.3
  4.6 0.0 copy-start.4
  4.6 0.7 copy-done.4
  5.3 0.0 copy-start.5
  5.3 0.7 copy-done.5
  5.9 45.1 %exchange.1 = (bf16[4,2048,256]{2,1,0:T(8,128)(2,1)S(1)}, bf16[4,2048,256]{2,1,0:T(8,128)(2,1)S(1)}, s32[72,256]{1,0:T(8,128)S(1)}, s32[64,128]{1,0:T(8,128)S(1)...) custom-call(bf16[2048,256]{1,0:T(8,128)(2,1)S(1)} %copy-done, s32[1,1,2,2048]{3,2,1,0:T(2,128)S(1)} %copy-done.1, ...), custom_call_target="tpu_custom_call" | custom-call | tf_op jit(solution)/shard_map/exchange/pallas_call | solution.py:198
  51.1 24.3 %edges.1 = bf16[2048,256]{1,0:T(8,128)(2,1)} custom-call(bf16[4,2048,256]{2,1,0:T(8,128)(2,1)S(1)} %get-tuple-element.11.own_ref, bf16[4,2048,256]{2,1,0:T(8,128)(2,1)S(1)} %get-tuple-element.12.prev_ref, s32[18432]{0:T(1024)S(1)} %bitcast.2, s32[64,128]{1,0:T(8,128)S(1)} %get-tuple-element.14.count_ref, f32[2048,128]{1,0:T(8,128)S(1)} %get-tuple-element.15.bank_ref, ...), custom_call_target="tpu_custom_call" | custom-call | tf_op jit(solution)/shard_map/edges/pallas_call | solution.py:386
  (1 shorter events, 0.0 us)
Async XLA Ops:
  1.2 1.2 %copy-start = (bf16[2048,256]{1,0:T(8,128)(2,1)S(1)}, bf16[2048,256]{1,0:T(8,128)(2,1)}, u32[]{:S(2)}) copy-start(bf16[2048,256]{1,0:T(8,128)(2,1)} %features.1) | copy-start | bytes 3145732
  2.4 0.7 copy-start.1
  3.1 0.7 copy-start.2
  3.9 0.7 copy-start.3
  4.6 0.7 copy-start.4
  5.3 0.7 copy-start.5

commit v3 on v2

--- a/solution.py
+++ b/solution.py
@@ -17,8 +17,9 @@
 
 
 def exchange_kernel(dims, features, source_ref, target_ref, map_ref, count_ref, restriction_ref, mixing_ref,
-                    own, prev, list_ref, live_ref, bank_ref, spread_ref,
-                    sources, targets, maps, counts, packed, position, home_sem, index_send, index_recv, send, recv):
+                    own, prev, near_table, far_table, list_ref, live_ref, bank_ref, spread_ref,
+                    sources, targets, maps, counts, restrictions, mixings, packed, position,
+                    home_sem, index_send, index_recv, send, recv):
     reps, blocks, rows, stalk, channels = dims
     width = stalk * channels
     half = width // 2
@@ -35,13 +36,17 @@
     to_next = {"rep": pair, "blk": after}
     from_last = {"rep": pair, "blk": before}
 
+    home = [pltpu.make_async_copy(src, dst, home_sem.at[k]) for k, (src, dst) in enumerate((
+        (source_ref, sources.at[rep]), (target_ref, targets.at[rep]), (map_ref, maps.at[rep]), (count_ref, counts.at[rep]),
+        (features, own.at[rep]), (restriction_ref, restrictions), (mixing_ref, mixings)))]
+    for copy in home:
+        copy.start()
+
     barrier = pltpu.get_barrier_semaphore()
     for other in (to_mate, to_pair, to_far, to_next, from_last):
         pl.semaphore_signal(barrier, inc=1, device_id=other, device_id_type=MESH)
     pl.semaphore_wait(barrier, 5)
 
-    home = pltpu.make_async_copy(features, own.at[rep], home_sem)
-    home.start()
     index_copies = []
     for a, (src, dst) in enumerate(((source_ref, sources), (target_ref, targets), (map_ref, maps), (count_ref, counts))):
         for k, other in enumerate((to_mate, to_pair, to_far)):
@@ -77,8 +82,8 @@
         to_next_own[k].start()
         to_mate_own[k].start()
 
-    for src, dst in ((source_ref, sources), (target_ref, targets), (map_ref, maps), (count_ref, counts)):
-        dst[rep] = src[...]
+    for copy in home:
+        copy.wait()
     for copy in index_copies:
         copy.wait_recv()
     steps, capacity = source_ref.shape[2:]
@@ -125,9 +130,6 @@
 
     lax.fori_loop(0, chunks, compress, 0)
 
-    count = restriction_ref.shape[0]
-    flat = restriction_ref[...].reshape(count * stalk, stalk)
-
     def three(x):
         high = x.astype(jnp.bfloat16)
         left = x - high.astype(jnp.float32)
@@ -139,31 +141,36 @@
             test(lax.broadcasted_iota(jnp.int32, shape, 0), lax.broadcasted_iota(jnp.int32, shape, 1)), 1.0, 0.0
         ).astype(jnp.bfloat16)
 
-    eye = ones((stalk, stalk), lambda p, q: p == q)
-    same = ones((width, width), lambda p, q: p // stalk == q // stalk)
-    wide = ones((width, width), lambda p, q: (p & (stalk - 1)) == q // channels)
-    flipped = [
-        lax.dot_general(eye, part, (((1,), (1,)), ((), ())), preferred_element_type=jnp.float32).astype(jnp.bfloat16)
-        for part in three(flat)]
-    per = width // stalk
-    for q in range(count // per):
-        total = jnp.zeros((width, width), jnp.float32)
-        for part in flipped:
-            stacked = jnp.concatenate([part[:, q * width:(q + 1) * width]] * per, axis=0) * same
-            total = total + jnp.dot(stacked, wide, preferred_element_type=jnp.float32)
-        for m in range(per):
-            for h in range(2):
-                for l in range(2):
-                    bank_ref[pl.ds(((q * per + m) * 4 + 2 * h + l) * 8, 8), :] = total[
-                        m * stalk + 8 * h:m * stalk + 8 * h + 8, l * half:(l + 1) * half]
+    count = restrictions.shape[2]
+    wide = ones((stalk, width), lambda p, q: p == q // channels)
+    for j in range(stalk):
+        total = jnp.zeros((count, width), jnp.float32)
+        for part in three(restrictions[:, j, :]):
+            total = total + lax.dot_general(part, wide, (((0,), (0,)), ((), ())), preferred_element_type=jnp.float32)
+        for l in range(2):
+            bank_ref[pl.ds(j // 8 * 16 + l * 8 + j % 8, count, stride=2 * stalk), :] = total[:, l * half:(l + 1) * half]
 
     tall = ones((width, channels), lambda p, q: (p & (channels - 1)) == q)
     broad = ones((channels, width), lambda p, q: p == (q & (channels - 1)))
     blocked = ones((width, width), lambda p, q: p // channels == q // channels)
-    for k, part in enumerate(three(mixing_ref[...])[:2]):
+    for k, part in enumerate(three(mixings[...])[:2]):
         part = jnp.dot(tall, part, preferred_element_type=jnp.float32).astype(jnp.bfloat16)
         spread_ref[k] = jnp.dot(part, broad, preferred_element_type=jnp.float32).astype(jnp.bfloat16) * blocked
 
+    def widen(block, table, shard, k):
+        def some(i, carry):
+            at = pl.multiple_of(k * piece + i * 128, 128)
+            rows_in = block[shard, pl.ds(at, 128), :].astype(jnp.float32)
+            table[pl.ds(pl.multiple_of(shard * rows + at, 128), 128), :] = rows_in[:, 0:half]
+            table[pl.ds(pl.multiple_of((reps + shard) * rows + at, 128), 128), :] = rows_in[:, half:width]
+            return carry
+
+        lax.fori_loop(0, piece // 128, some, 0)
+
+    for k in every:
+        to_mate_own[k].wait_recv()
+        widen(own, near_table, rep, k)
+        widen(own, near_table, mate, k)
     for k in every:
         to_pair_own[k].wait_recv()
         mate_pairs[k].start()
@@ -173,15 +180,32 @@
         mate_lasts[k].start()
         if k in second:
             pair_lasts[k - PIECES // 2].start()
+        widen(own, near_table, pair, k)
+        widen(prev, far_table, pair, k)
+        if k > 0:
+            mate_pairs[k - 1].wait_recv()
+            mate_lasts[k - 1].wait_recv()
+            widen(own, near_table, far, k - 1)
+            widen(prev, far_table, far, k - 1)
     for k in first:
         next_pairs[k].wait_recv()
         mate_rest[k].start()
         pair_lasts[k].wait_recv()
         mate_rest[k + PIECES // 2].start()
-    for family in (to_mate_own, mate_pairs, mate_lasts, mate_rest):
-        for copy in family:
-            copy.wait_recv()
-    home.wait()
+        if k == 0:
+            mate_pairs[PIECES - 1].wait_recv()
+            mate_lasts[PIECES - 1].wait_recv()
+            widen(own, near_table, far, PIECES - 1)
+            widen(prev, far_table, far, PIECES - 1)
+        else:
+            for j in (k - 1, k - 1 + PIECES // 2):
+                mate_rest[j].wait_recv()
+                widen(prev, far_table, mate, j)
+        widen(prev, far_table, rep, k)
+        widen(prev, far_table, rep, k + PIECES // 2)
+    for j in (PIECES // 2 - 1, PIECES - 1):
+        mate_rest[j].wait_recv()
+        widen(prev, far_table, mate, j)
     for copy in index_copies:
         copy.wait_send()
     for family in (to_mate_own, to_pair_own, to_next_own, mate_pairs, mate_lasts, next_pairs, pair_lasts, mate_rest):
@@ -193,36 +217,42 @@
     reps, blocks, rows, stalk, channels = dims
     width = stalk * channels
     chunks = reps * sources.size // SLOTS
+    restriction = jnp.transpose(restriction, (1, 2, 0))
+    operands = [pltpu.with_memory_space_constraint(x, pltpu.HBM) for x in (
+        features, sources, targets, maps, counts, restriction, mixing)]
     vmem = pl.BlockSpec(memory_space=pltpu.VMEM)
-    block = jax.ShapeDtypeStruct((reps, rows, width), features.dtype)
     return pl.pallas_call(
         functools.partial(exchange_kernel, dims),
         out_shape=(
-            block,
-            block,
-            jax.ShapeDtypeStruct((chunks + 8, SLOTS), jnp.int32),
-            jax.ShapeDtypeStruct((chunks, 128), jnp.int32),
-            jax.ShapeDtypeStruct((2 * restriction.shape[0] * stalk, width // 2), jnp.float32),
-            jax.ShapeDtypeStruct((2, width, width), jnp.bfloat16),
+            pltpu.VMEM((reps, rows, width), features.dtype),
+            pltpu.VMEM((reps, rows, width), features.dtype),
+            pltpu.VMEM((2 * reps * rows, width // 2), jnp.float32),
+            pltpu.VMEM((2 * reps * rows, width // 2), jnp.float32),
+            pltpu.VMEM((chunks + 8, SLOTS), jnp.int32),
+            pltpu.VMEM((chunks, 128), jnp.int32),
+            pltpu.VMEM((2 * restriction.shape[2] * stalk, width // 2), jnp.float32),
+            pltpu.VMEM((2, width, width), jnp.bfloat16),
         ),
-        in_specs=[pl.BlockSpec(memory_space=pl.ANY)] + [vmem] * 6,
-        out_specs=(vmem,) * 6,
+        in_specs=[pl.BlockSpec(memory_space=pltpu.HBM)] * 7,
+        out_specs=(vmem,) * 8,
         scratch_shapes=[
             pltpu.VMEM((reps, *sources.shape), jnp.int32),
             pltpu.VMEM((reps, *sources.shape), jnp.int32),
             pltpu.VMEM((reps, *sources.shape), jnp.int32),
             pltpu.VMEM((reps, *counts.shape), jnp.int32),
+            pltpu.VMEM(restriction.shape, restriction.dtype),
+            pltpu.VMEM(mixing.shape, mixing.dtype),
             pltpu.VMEM((chunks, SLOTS), jnp.int32),
             pltpu.VMEM((chunks, SLOTS), jnp.int32),
-            pltpu.SemaphoreType.DMA,
+            pltpu.SemaphoreType.DMA((7,)),
             pltpu.SemaphoreType.DMA((4, 3)),
             pltpu.SemaphoreType.DMA((4, 3)),
             pltpu.SemaphoreType.DMA((8, PIECES)),
             pltpu.SemaphoreType.DMA((8, PIECES)),
         ],
-        compiler_params=pltpu.CompilerParams(collective_id=0, has_side_effects=True, vmem_limit_bytes=28 << 20),
+        compiler_params=pltpu.CompilerParams(collective_id=0, has_side_effects=True, vmem_limit_bytes=8 << 20),
         name="exchange",
-    )(features, sources, targets, maps, counts, restriction, mixing)
+    )(*operands)
 
 
 def column_sums(parts, sub):
@@ -238,8 +268,8 @@
     return parts[0]
 
 
-def edge_kernel(dims, own_ref, prev_ref, list_ref, count_ref, bank_ref, spread_ref, out_ref,
-                table, ring_even, ring_odd, starts, *rest):
+def edge_kernel(dims, own_ref, near_table, far_table, list_ref, count_ref, bank_ref, spread_ref, out_ref,
+                ring_even, ring_odd, starts, *rest):
     reps, rows, width, steps, chunks, slots = dims
     accs = rest
     half = width // 2
@@ -259,16 +289,7 @@
     n_at = lax.broadcasted_iota(jnp.int32, (width, width), 1)
     repeat = jnp.where((k_at % 16 == n_at % 16) & (k_at // half == n_at // half), 1.0, 0.0).astype(jnp.bfloat16)
     for turn in range(steps):
-        for shard in range(reps):
-            def widen(i, _, shard=shard, turn=turn):
-                src = pl.ds(pl.multiple_of(i * 128, 128), 128)
-                dst = pl.ds(pl.multiple_of(shard * rows + i * 128, 128), 128)
-                wide = (own_ref, prev_ref)[turn][shard, src, :].astype(jnp.float32)
-                table[dst, :] = wide[:, 0:half]
-                table[pl.ds(pl.multiple_of((reps + shard) * rows + i * 128, 128), 128), :] = wide[:, half:width]
-                return 0
-            lax.fori_loop(0, rows // 128, widen, 0)
-        per = chunks // (reps * steps)
+        table = (near_table, far_table)[turn]
 
         def plan(c, filled, turn=turn):
             at = c * steps + turn
@@ -377,7 +398,7 @@
     pl.run_scoped(mix, *[pltpu.ACC(side)((block, width), jnp.float32) for side in range(2)])
 
 
-def edges(own, prev, lists, counts, bank, spread):
+def edges(own, near, far, lists, counts, bank, spread):
     reps, rows, width = own.shape
     chunks = counts.shape[0]
     dims = (reps, rows, width, 2, chunks, SLOTS)
@@ -386,18 +407,17 @@
     return pl.pallas_call(
         functools.partial(edge_kernel, dims),
         out_shape=jax.ShapeDtypeStruct((rows, width), own.dtype),
-        in_specs=[vmem, vmem, smem, smem, vmem, vmem],
+        in_specs=[vmem, vmem, vmem, smem, smem, vmem, vmem],
         out_specs=vmem,
         scratch_shapes=[
-            pltpu.VMEM((2 * reps * rows, width // 2), jnp.float32),
             pltpu.VMEM((2 * GROUP, width // 2), jnp.float32),
             pltpu.VMEM((2 * GROUP, width // 2), jnp.float32),
             pltpu.SMEM((lists.shape[0] // 8 + 16,), jnp.int32),
             *[pltpu.VMEM((2 * rows + 128, width // 2), jnp.float32)] * ACCS,
         ],
-        compiler_params=pltpu.CompilerParams(vmem_limit_bytes=36 << 20),
+        compiler_params=pltpu.CompilerParams(vmem_limit_bytes=16 << 20),
         name="edges",
-    )(own, prev, lists, counts, bank, spread)
+    )(own, near, far, lists, counts, bank, spread)
 
 
 def body(features, restriction, mixing, source_index, target_index, map_index, edge_counts):
@@ -405,9 +425,9 @@
     stalk = restriction.shape[1]
     channels = mixing.shape[0]
     dims = (lax.axis_size("rep"), lax.axis_size("blk"), rows, stalk, channels)
-    own, prev, lists, counts, bank, spread = exchange(
+    own, _, near, far, lists, counts, bank, spread = exchange(
         dims, features, source_index, target_index, map_index, edge_counts, restriction, mixing)
-    return edges(own, prev, lists.reshape(-1), counts, bank, spread)
+    return edges(own, near, far, lists.reshape(-1), counts, bank, spread)
 
 
 def solution(mesh):

time: 76 us -> 71.4 us (0.939)
  the two profiles are of different devices: /device:TPU:49 before, /device:TPU:1 now
where the time goes in v3:
time: 71.4 us; the launch traced here: 70.4 us
  Pallas kernels  70.4 us (99%)
    pallas_call x1, Pallas kernels, exchange(): pl.pallas_call(functools.partial(exchange_kernel, dims), out_shape=(pltpu...  50.4 us
    pallas_call x1, Pallas kernels, edges(): pl.pallas_call(functools.partial(edge_kernel, dims), out_shape=jax.ShapeD...  20 us

profile of v3, /device:TPU:1, one launch (start us, length us, event | category | flops | bytes accessed | tf_op | source)
XLA Modules:
  0.0 70.4 jit_solution(3868042490641782545)
XLA Ops:
  0.0 50.4 %exchange.1 = (bf16[4,2048,256]{2,1,0:T(8,128)(2,1)S(1)}, bf16[4,2048,256]{2,1,0:T(8,128)(2,1)}, f32[16384,128]{1,0:T(8,128)S(1)}, f32[16384,128]{1,0:T(8,128)S(...) custom-call(bf16[2048,256]{1,0:T(8,128)(2,1)} %features.1, ...), custom_call_target="tpu_custom_call" | custom-call | tf_op jit(solution)/shard_map/exchange/pallas_call | solution.py:224
  50.4 20.0 %edges.1 = bf16[2048,256]{1,0:T(8,128)(2,1)} custom-call(bf16[4,2048,256]{2,1,0:T(8,128)(2,1)S(1)} %get-tuple-element.12.own_ref, f32[16384,128]{1,0:T(8,128)S(1)} %get-tuple-element.13.near_table, f32[16384,128]{1,0:T(8,128)S(1)} %get-tuple-element.14.far_table, s32[18432]{0:T(1024)S(1)} %bitcast.3, s32[64,128]{1,0:T(8,128)S(1)} %get-tuple-element.16.count_ref, ...), custom_call_target="tpu_custom_call" | custom-call | tf_op jit(solution)/shard_map/edges/pallas_call | solution.py:407
  (1 shorter events, 0.0 us)
